TPU v7x, 256 devices: a whole 4x4x8 slice. The times are simulated.
256 devices in a mesh: real: 16 (over x_hi, y, core), site: 16 (over x_lo, z).
Axes of the slice: x: 4 (x_hi: 2, x_lo: 2; x = x_hi * 2 + x_lo), y: 4, z: 8, core: 2. Of those that a mesh axis runs over, the one named last changes fastest.
Arguments:
- noise: bfloat16 [16384, 12288], P('site', 'real'), may hold values from -6 to 6
- v_factors: bfloat16 [16, 1024, 4096], P('site', 'real'), may hold values from -0.1875 to 0.1875
- u_factors: bfloat16 [16, 1024, 4096], P('site', 'real'), may hold values from -0.09375 to 0.09375
- ranks: int32 [16, 16], replicated, may hold values from 1 to 2, as said below
- skew_g: float32 [16384], P('site'), may hold values from 0.1 to 0.6
- tail_h: float32 [16384], P('site'), may hold values from 0.05 to 0.3
Outputs:
- field: float32 [16384, 12288], P('site', 'real')
Inputs may be any that keep to these rules, and one draw needn't show every extreme that they name: `ranks`: every tile has at least one rank block, and some tile has 2.
All inputs are finite; a program needn't handle non-finite values.
Results may differ from a plain program's by a relative error of at most 0.012.
The roundings to bfloat16 on the way count: a program that leaves them out, or rounds other values in their place, can miss the bound.
Values may be sent and summed in bfloat16 or wider, within the bound.
A program may use at most 128 MiB of HBM per device.

v0:
```python
import jax
import jax.numpy as jnp
from jax import lax
from jax.sharding import PartitionSpec as P

CAP = 2


def per_device(noise, v_factors, u_factors, ranks, skew_g, tail_h):
    group_count = lax.axis_size("site")
    myself = lax.axis_index("site")
    columns = v_factors.shape[2]
    per_dest = columns // group_count
    real_count = noise.shape[1]
    groups = jnp.arange(group_count, dtype=jnp.int32)
    own_column = jnp.sum(jnp.where(groups[None, :] == myself, ranks, 0), axis=1)
    levels = jnp.arange(CAP, dtype=jnp.int32)
    alive = (levels[None, :] < own_column[:, None]).astype(jnp.float32)
    v_whole = lax.all_gather(v_factors, "real", axis=1, tiled=True)[0]
    projected = lax.dot_general(
        v_whole, noise, (((0,), (0,)), ((), ())), preferred_element_type=jnp.float32
    )
    masked = (
        projected.reshape(group_count, CAP, per_dest // CAP, real_count) * alive[:, :, None, None]
    )
    sending = masked.astype(jnp.bfloat16).reshape(group_count, per_dest, real_count)
    received = lax.all_to_all(sending, "site", split_axis=0, concat_axis=0, tiled=True)
    flattened = received.reshape(columns, real_count)
    gaussian = jnp.dot(
        lax.all_gather(u_factors, "real", axis=1, tiled=True)[0],
        flattened,
        preferred_element_type=jnp.float32,
    )
    skew_col = skew_g[:, None]
    tail_col = tail_h[:, None]
    return jnp.expm1(skew_col * gaussian) / skew_col * jnp.exp(0.5 * tail_col * gaussian * gaussian)


def solution(mesh):
    placed = (
        P("site", "real"),
        P("site", "real", None),
        P("site", "real", None),
        P(),
        P("site"),
        P("site"),
    )
    return jax.shard_map(
        per_device, mesh=mesh, in_specs=placed, out_specs=P("site", "real"), check_vma=False
    )
```

profile of v0, /device:TPU:4, one launch (start us, length us, event | category | flops | bytes accessed | tf_op | source)
XLA Modules:
  0.0 285.7 jit_solution(5475105755037415597)
XLA Ops:
  6.5 0.0 copy-start
  6.5 0.0 all-gather.3.cloned.1.call-start
  6.5 0.7 all-gather.3.cloned.1.call-update
  7.3 0.0 all-gather.5.cloned.1.call-start
  7.3 0.7 all-gather.5.cloned.1.call-update
  8.0 0.8 select_reduce_fusion
  8.8 0.1 fusion.9
  8.9 79.4 %all-gather.3.cloned.1.call-done = bf16[1,1024,4096]{2,1,0:T(8,128)(2,1)} async-done(((bf16[1,64,4096]{2,1,0:T(8,128)(2,1)}), bf16[1,1024,4096]{2,1,0:T(8,128)(2,1)}) %all-gather.3.cloned.1.call-update) | async-done | bytes 8388624 | tf_op jit(solution)/shard_map/all_gather | solution.py:19
  88.3 12.0 %copy.7 = bf16[4096,1024]{1,0:T(8,128)(2,1)} copy(bf16[4096,1024]{0,1:T(8,128)(2,1)} %bitcast.27) | data formatting | bytes 16777216 | tf_op jit(solution)/shard_map/dot_general | solution.py:20
  100.3 0.0 copy-done
  100.3 11.9 %multiply_convert_fusion = bf16[16,2,128,768]{3,2,1,0:T(8,128)(2,1)} fusion(f32[16,2]{1,0:T(8,128)S(1)} %fusion.9, bf16[16,2,128,1024]{3,2,1,0:T(8,128)(2,1)} %bitcast.28, bf16[1024,768]{1,0:T(8,128)(2,1)S(1)} %copy-done), kind=kOutput, calls=%fused_computation | convolution fusion | flops 6448742400 | bytes 16253056 | tf_op jit(solution)/shard_map/dot_general | solution.py:20
  112.3 0.0 copy-start.1
  112.3 0.0 copy-start.2
  112.3 9.0 %all-to-all-start = ((bf16[16,256,768]{2,1,0:T(8,128)(2,1)}), bf16[16,256,768]{2,1,0:T(8,128)(2,1)}, u32[]{:S(2)}, u32[]{:S(2)}) async-start(bf16[16,256,768]{2,1,0:T(8,128)(2,1)} %bitcast.29), calls=%async_computation | async-start | bytes 12582912 | tf_op jit(solution)/shard_map/all_to_all | solution.py:27
  121.3 0.0 copy-done.1
  121.3 63.0 %all-gather.5.cloned.1.call-done = bf16[1,1024,4096]{2,1,0:T(8,128)(2,1)} async-done(((bf16[1,64,4096]{2,1,0:T(8,128)(2,1)}), bf16[1,1024,4096]{2,1,0:T(8,128)(2,1)}) %all-gather.5.cloned.1.call-update) | async-done | bytes 8388624 | tf_op jit(solution)/shard_map/all_gather | solution.py:30
  184.3 77.5 %all-to-all-done = bf16[16,256,768]{2,1,0:T(8,128)(2,1)} async-done(((bf16[16,256,768]{2,1,0:T(8,128)(2,1)}), bf16[16,256,768]{2,1,0:T(8,128)(2,1)}, u32[]{:S(2)}, u32[]{:S(2)}) %all-to-all-start) | async-done | bytes 6291488 | tf_op jit(solution)/shard_map/all_to_all | solution.py:27
  261.9 0.0 copy-done.2
  261.9 13.4 %fusion.3 = f32[1024,768]{0,1:T(8,128)} fusion(bf16[4096,768]{1,0:T(8,128)(2,1)} %bitcast.6, bf16[1,1024,4096]{2,1,0:T(8,128)(2,1)} %all-gather.5.cloned.1.call-done, f32[1024]{0:T(1024)S(1)} %broadcast_multiply_fusion, f32[1024]{0:T(1024)S(1)} %copy-done.2), kind=kOutput, calls=%fused_computation.5 | convolution fusion | flops 6446383104 | bytes 17833984 | tf_op jit(solution)/shard_map/dot_general | solution.py:29
  275.3 3.5 %copy.8 = f32[1024,768]{1,0:T(8,128)} copy(f32[1024,768]{0,1:T(8,128)} %fusion.3) | data formatting | bytes 6291456 | tf_op jit(solution)/shard_map/mul | solution.py:36
  (2 shorter events, 0.0 us)
Async XLA Ops:
  6.5 93.8 %copy-start = (bf16[1024,768]{1,0:T(8,128)(2,1)S(1)}, bf16[1024,768]{1,0:T(8,128)(2,1)}, u32[]{:S(2)}) copy-start(bf16[1024,768]{1,0:T(8,128)(2,1)} %param.6) | copy-start | bytes 4718596
  6.5 81.8 %all-gather.3.cloned.1.call-start = ((), (), s32[]{:S(2)}) async-start(), calls=%async_computation.1 | async-start | bytes 8912896 | tf_op jit(solution)/shard_map/all_gather | solution.py:19
  7.3 177.1 %all-gather.5.cloned.1.call-start = ((), (), s32[]{:S(2)}) async-start(), calls=%async_computation.2 | async-start | bytes 8912896 | tf_op jit(solution)/shard_map/all_gather | solution.py:30
  112.3 9.0 %copy-start.1 = (f32[1024]{0:T(1024)S(1)}, f32[1024]{0:T(1024)}, u32[]{:S(2)}) copy-start(f32[1024]{0:T(1024)} %param.11) | copy-start | bytes 12292
  112.3 149.6 %copy-start.2 = (f32[1024]{0:T(1024)S(1)}, f32[1024]{0:T(1024)}, u32[]{:S(2)}) copy-start(f32[1024]{0:T(1024)} %param.10) | copy-start | bytes 12292
  112.3 149.6 %all-to-all-start = ((bf16[16,256,768]{2,1,0:T(8,128)(2,1)}), bf16[16,256,768]{2,1,0:T(8,128)(2,1)}, u32[]{:S(2)}, u32[]{:S(2)}) async-start(bf16[16,256,768]{2,1,0:T(8,128)(2,1)} %bitcast.29), calls=%async_computation | async-start | bytes 12582912 | tf_op jit(solution)/shard_map/all_to_all | solution.py:27
Sparse Core Ops, SparseCore 0:
  10.1 78.1 all-gather.2
  91.1 93.2 all-gather.4
where the time goes:
time: 288 us; the launch traced here: 286 us
  waiting for transfers between devices  221 us (77%)
  matrix products  25.3 us (9%)
  local copies, waits for them, and re-layouts  15.6 us (5%)
  between operations  13.4 us (5%)
  starting transfers between devices  9.07 us (3%)
    all_gather x1, waiting for transfers between devices, per_device(): v_whole = lax.all_gather(v_factors, 'real', axis=1, tiled=True)[0]  79.4 us
    all_to_all x1, waiting for transfers between devices, per_device(): lax.all_to_all(sending, 'site', split_axis=0, concat_axis=0, tiled=True)  77.5 us
    all_gather x1, waiting for transfers between devices, per_device(): lax.all_gather(u_factors, 'real', axis=1, tiled=True)[0]  63 us
    dot_general x1, matrix products, per_device(): jnp.dot(lax.all_gather(u_factors, 'real', axis=1, tiled=True)[0], flatten...  13.4 us
    dot_general x1, local copies, waits for them, and re-layouts, per_device(): lax.dot_general(v_whole, noise, (((0,), (0,)), ((), ())), preferred_eleme...  12 us
    dot_general x1, matrix products, per_device(): lax.dot_general(v_whole, noise, (((0,), (0,)), ((), ())), preferred_eleme...  11.9 us
    all_to_all x1, starting transfers between devices, per_device(): lax.all_to_all(sending, 'site', split_axis=0, concat_axis=0, tiled=True)  9.03 us
  transfers between devices with their start and end apart: 3, of which 3 were waited for; matrix products, arithmetic and copies ran while one was open for 9% of the time, Pallas kernels for 0%

commit v1 on v0

v1 whole, which is shorter than its diff:
```python
import functools

import jax
import jax.numpy as jnp
from jax import lax
from jax.experimental import pallas as pl
from jax.experimental.pallas import tpu as pltpu
from jax.sharding import PartitionSpec as P

MESH = pl.DeviceIdType.MESH
CAP = 2
ZS = 8
YS = 4
CHUNKS = 3

SLOTS = (
    (0, 1, 0), (1, 1, 0), (-1, 1, 0), (2, 1, 0), (-2, 1, 0),
    (-2, 0, 1), (-2, 1, 1), (2, 0, -1),
    (2, 1, -1), (-2, 0, 2), (2, 1, -2),
    (0, 0, 0), (1, 0, 0), (-1, 0, 0), (2, 0, 0), (-2, 0, 0),
)
SENT = 11
EARLY = ((0, 5), (11, 16))
LATE = (5, 11)
AT = {0: 0, 1: 1, -1: 2, 2: 3, -2: 4}
HALVES = 2


def tukey(x, g, h):
    y = g * x
    series = y * (1.0 + y * (0.5 + y * (1.0 / 6 + y * (1.0 / 24 + y * (1.0 / 120 + y * (1.0 / 720 + y * (1.0 / 5040)))))))
    lifted = jnp.where(jnp.abs(y) < 0.35, series, jnp.exp(y) - 1.0)
    return lifted / g * jnp.exp(0.5 * h * x * x)


def kernel(noise, v, u, ranks, skew, tail, out, nt, gv, gu, cs, cr, gb, hb, vs, vr, as_, ar, ns, nr, ps, pr, local):
    real, site = lax.axis_index("real"), lax.axis_index("site")
    core = lax.rem(real, 2)
    y = lax.rem(lax.div(real, 2), YS)
    xh = lax.div(real, 2 * YS)
    x = lax.div(site, ZS)
    z = lax.rem(site, ZS)
    rows = v.shape[0]
    unit = v.shape[1] // len(SLOTS)
    rank_block = unit // CAP
    piece = noise.shape[1] // CHUNKS

    def site_of(fx, dz):
        return (1 - x if fx else x) * ZS + lax.rem(z + dz + ZS, ZS)

    def real_of(fh, dy, fc):
        hi = 1 - xh if fh else xh
        lo = 1 - core if fc else core
        return (hi * YS + lax.rem(y + dy + YS, YS)) * 2 + lo

    def cols(index):
        return pl.ds(pl.multiple_of(index * unit, unit), unit)

    def fixed(index):
        return pl.ds(index * unit, unit)

    def part(c):
        return pl.ds(c * piece, piece)

    barrier = pltpu.get_barrier_semaphore()
    peers = [(real, site_of(0, d)) for d in (1, -1, 2, -2)]
    peers += [(real, site_of(1, d)) for d in (0, 1, -1, 2, -2)]
    peers += [(real_of(*w), site) for w in ((1, 0, 0), (0, 1, 0), (0, -1, 0), (0, 0, 1))]
    for peer in peers:
        pl.semaphore_signal(barrier, inc=1, device_id=peer, device_id_type=MESH)
    pl.semaphore_wait(barrier, len(peers))

    mine = pl.ds(pl.multiple_of(real * rows, rows), rows)

    def v_copy(m):
        dj, fx, di = SLOTS[m]
        wanted = cols(site_of(fx, di - dj))
        if dj == 0:
            return pltpu.make_async_copy(v.at[:, wanted], gv.at[mine, fixed(m)], local.at[m])
        return pltpu.make_async_remote_copy(
            src_ref=v.at[:, wanted], dst_ref=gv.at[mine, fixed(m)], send_sem=vs.at[m], recv_sem=vr.at[m],
            device_id=(real, site_of(0, -dj)), device_id_type=MESH,
        )

    v_copies = [v_copy(m) for m in range(len(SLOTS))]
    for copy in v_copies:
        copy.start()

    u_copies = []
    for m, (dj, fx, di) in enumerate(SLOTS):
        u_copies.append(
            pltpu.make_async_copy(u.at[:, cols(site_of(fx, dj - di))], gu.at[mine, fixed(m)], local.at[len(SLOTS) + m])
        )
        u_copies[-1].start()

    KINDS = (
        ((0, 0), (1, 0, 0)),
        ((0, 0), (0, 1, 0)), ((0, 0), (0, -1, 0)),
        ((1, 0), (0, 1, 0)), ((1, 0), (0, -1, 0)),
        ((0, -1), (0, 1, 0)), ((1, 1), (0, -1, 0)),
    ) + tuple((block, (0, 0, 1)) for block in ((0, 0), (1, 0), (0, -1), (0, 1), (1, -1), (1, 1), (0, 2), (1, 2)))

    def gather(buffer, which, half):
        width = buffer.shape[1] // HALVES
        copies = []
        for kind, ((fh, dy), to) in enumerate(KINDS):
            owner = real_of(fh, dy, 0)
            block = buffer.at[pl.ds(pl.multiple_of(owner * rows, rows), rows), pl.ds(half * width, width)]
            index = (which * HALVES + half) * len(KINDS) + kind
            copies.append(
                pltpu.make_async_remote_copy(
                    src_ref=block, dst_ref=block, send_sem=as_.at[index], recv_sem=ar.at[index],
                    device_id=(real_of(*to), site), device_id_type=MESH,
                )
            )
        return copies

    def start(copies, *kinds):
        for kind in kinds:
            copies[kind].start()

    def step(copies, number):
        if number == 0:
            start(copies, 0, 1, 2, 7)
        elif number == 1:
            copies[0].wait_recv()
            start(copies, 3, 4, 8)
        elif number == 2:
            copies[1].wait_recv()
            start(copies, 5, 9)
            copies[2].wait_recv()
            start(copies, 10)
        elif number == 3:
            copies[4].wait_recv()
            start(copies, 6, 12)
            copies[3].wait_recv()
            start(copies, 11)
        elif number == 4:
            copies[5].wait_recv()
            start(copies, 13)
            copies[6].wait_recv()
            start(copies, 14)
        else:
            for kind in range(7, 15):
                copies[kind].wait_recv()

    va, vb = gather(gv, 0, 0), gather(gv, 0, 1)
    ua, ub = gather(gu, 1, 0), gather(gu, 1, 1)

    def noise_copy(c, way, hop):
        return pltpu.make_async_remote_copy(
            src_ref=nt.at[0 if hop == 0 else AT[-way], part(c)],
            dst_ref=nt.at[AT[-way * (hop + 1)], part(c)],
            send_sem=ns.at[(c * 2 + (way > 0)) * 2 + hop], recv_sem=nr.at[(c * 2 + (way > 0)) * 2 + hop],
            device_id=(real, site_of(0, way)), device_id_type=MESH,
        )

    noise_copies = {(c, way, hop): noise_copy(c, way, hop) for c in range(CHUNKS) for way in (1, -1) for hop in (0, 1)}

    def turn(c):
        nt[0, part(c), :] = noise[:, part(c)].T

    def first(c):
        for way in (1, -1):
            noise_copies[c, way, 0].start()

    def forward(c):
        for way in (1, -1):
            noise_copies[c, way, 0].wait_recv()
            noise_copies[c, way, 1].start()

    def far(c):
        for way in (1, -1):
            noise_copies[c, way, 1].wait_recv()

    turn(0)
    turn(1)
    first(0)
    turn(2)
    first(1)

    for copy in u_copies:
        copy.wait()
    step(ua, 0)

    for m in range(len(SLOTS)):
        if SLOTS[m][0] == 0:
            v_copies[m].wait()
        else:
            v_copies[m].wait_recv()
        if m == len(SLOTS) // HALVES - 1:
            step(va, 0)
    step(vb, 0)

    for k in range(skew.shape[0]):
        spread = pl.ds(k * 128, 128)
        gb[spread, :] = jnp.broadcast_to(skew[pl.ds(k, 1), :], (128, 128)).T
        hb[spread, :] = jnp.broadcast_to(tail[pl.ds(k, 1), :], (128, 128)).T

    def coef_copy(m, c):
        dj, fx, di = SLOTS[m]
        return pltpu.make_async_remote_copy(
            src_ref=cs.at[part(c), fixed(m)], dst_ref=cr.at[part(c), fixed(m)],
            send_sem=ps.at[m * CHUNKS + c], recv_sem=pr.at[m * CHUNKS + c],
            device_id=(real, site_of(fx, di)), device_id_type=MESH,
        )

    coef_copies = {(m, c): coef_copy(m, c) for m in range(SENT) for c in range(CHUNKS)}
    level = lax.broadcasted_iota(jnp.int32, (1, unit), 1) // rank_block

    def project(m, c):
        dj, fx, di = SLOTS[m]
        projected = jnp.dot(nt[AT[dj], part(c), :], gv[:, fixed(m)], preferred_element_type=jnp.float32)
        alive = (level < ranks[site_of(fx, di), site_of(0, dj)]).astype(jnp.float32)
        (cs if m < SENT else cr)[part(c), fixed(m)] = (projected * alive).astype(jnp.bfloat16)

    def projects(*tasks):
        waiting = None
        for task in tasks:
            project(*task)
            if waiting is not None:
                coef_copies[waiting].start()
            waiting = task if task[0] < SENT else None
        if waiting is not None:
            coef_copies[waiting].start()

    def dot_t(left, right):
        return lax.dot_general(left, right, (((1,), (1,)), ((), ())), preferred_element_type=jnp.float32)

    block = 256

    def early(c):
        @pl.loop(0, out.shape[0] // block)
        def _(k):
            here = pl.ds(pl.multiple_of(k * block, block), block)
            total = None
            for lo, hi in EARLY:
                span = pl.ds(lo * unit, (hi - lo) * unit)
                term = dot_t(gu[here, span], cr[part(c), span])
                total = term if total is None else total + term
            out[here, part(c)] = total

    def late(c):
        @pl.loop(0, out.shape[0] // block)
        def _(k):
            here = pl.ds(pl.multiple_of(k * block, block), block)
            span = pl.ds(LATE[0] * unit, (LATE[1] - LATE[0]) * unit)
            total = out[here, part(c)] + dot_t(gu[here, span], cr[part(c), span])
            g, h = gb[here, :], hb[here, :]
            for q in range(piece // 128):
                out[here, pl.ds(c * piece + q * 128, 128)] = tukey(total[:, q * 128:(q + 1) * 128], g, h)

    def arrived(slots, c):
        for m in slots:
            coef_copies[m, c].wait_recv()

    step(va, 1)
    step(va, 2)
    forward(0)
    first(2)
    step(vb, 1)
    step(va, 3)
    step(vb, 2)
    step(va, 4)
    step(va, 5)
    projects((0, 0), (0, 1), (0, 2))
    forward(1)
    projects((1, 0), (2, 0), (1, 1), (2, 1))
    step(vb, 3)
    step(ua, 1)
    step(ub, 0)
    step(vb, 4)
    step(vb, 5)
    step(ua, 2)
    far(0)
    projects((5, 0), (6, 0), (7, 0), (8, 0), (9, 0), (10, 0), (3, 0), (4, 0))
    step(ub, 1)
    projects((11, 0), (12, 0), (13, 0), (14, 0), (15, 0))
    step(ua, 3)
    projects((11, 1), (12, 1), (13, 1), (11, 2))
    forward(2)
    projects((1, 2), (2, 2), (12, 2), (13, 2))
    step(ub, 2)
    step(ua, 4)
    far(1)
    projects((5, 1), (6, 1), (7, 1), (8, 1), (9, 1), (10, 1), (3, 1), (4, 1), (14, 1), (15, 1))
    step(ub, 3)
    step(ub, 4)
    step(ua, 5)
    step(ub, 5)
    arrived(range(5), 0)
    early(0)
    arrived(range(5, SENT), 0)
    late(0)
    far(2)
    projects((5, 2), (6, 2), (7, 2), (8, 2), (9, 2), (10, 2), (3, 2), (4, 2), (14, 2), (15, 2))
    arrived(range(5), 1)
    early(1)
    arrived(range(5, SENT), 1)
    late(1)
    arrived(range(5), 2)
    early(2)
    arrived(range(5, SENT), 2)
    late(2)

    for m, copy in enumerate(v_copies):
        if SLOTS[m][0] != 0:
            copy.wait_send()
    for copies in (va, vb, ua, ub):
        for copy in copies:
            copy.wait_send()
    for copy in noise_copies.values():
        copy.wait_send()
    for copy in coef_copies.values():
        copy.wait_send()


def per_device(noise, v_factors, u_factors, ranks, skew_g, tail_h):
    v, u = v_factors[0], u_factors[0]
    tile, count = noise.shape
    columns = v.shape[1]
    vmem = pl.BlockSpec(memory_space=pltpu.VMEM)
    dma = pltpu.SemaphoreType.DMA
    gathers = 2 * HALVES * 15
    return pl.pallas_call(
        kernel,
        out_shape=jax.ShapeDtypeStruct((tile, count), jnp.float32),
        in_specs=[vmem, vmem, vmem, pl.BlockSpec(memory_space=pltpu.SMEM), vmem, vmem],
        out_specs=vmem,
        scratch_shapes=[
            pltpu.VMEM((5, count, tile), jnp.bfloat16),
            pltpu.VMEM((tile, columns), jnp.bfloat16),
            pltpu.VMEM((tile, columns), jnp.bfloat16),
            pltpu.VMEM((count, columns // len(SLOTS) * SENT), jnp.bfloat16),
            pltpu.VMEM((count, columns), jnp.bfloat16),
            pltpu.VMEM((tile, 128), jnp.float32),
            pltpu.VMEM((tile, 128), jnp.float32),
            dma((16,)), dma((16,)),
            dma((gathers,)), dma((gathers,)),
            dma((4 * CHUNKS,)), dma((4 * CHUNKS,)),
            dma((SENT * CHUNKS,)), dma((SENT * CHUNKS,)),
            dma((32,)),
        ],
        compiler_params=pltpu.CompilerParams(
            collective_id=0, has_side_effects=True, vmem_limit_bytes=60 * 1024 * 1024
        ),
    )(noise, v, u, ranks, skew_g.reshape(-1, 128), tail_h.reshape(-1, 128))


def solution(mesh):
    placed = (
        P("site", "real"),
        P("site", "real", None),
        P("site", "real", None),
        P(),
        P("site"),
        P("site"),
    )
    return jax.shard_map(
        per_device, mesh=mesh, in_specs=placed, out_specs=P("site", "real"), check_vma=False
    )
```

time: 288 us -> 139 us (0.48)
  waiting for transfers between devices: 221 us -> 0 us
  Pallas kernels: 0 us -> 134 us
  matrix products: 25.3 us -> 0 us
  between operations: 13.4 us -> 0.01 us
  local copies, waits for them, and re-layouts: 15.6 us -> 3.76 us
  starting transfers between devices: 9.07 us -> 0 us
    all_gather x2 -> x0, waiting for transfers between devices: 142 us -> none  [the longest x1 79.4 us: per_device(): v_whole = lax.all_gather(v_factors, 'real', axis=1, tiled=True)[0]]
    pallas_call x0 -> x1, Pallas kernels: none -> 134 us  [per_device(): pl.pallas_call(kernel, out_shape=jax.ShapeDtypeStruct((tile, count), jnp....]
    all_to_all x1 -> x0, waiting for transfers between devices: 77.5 us -> none  [per_device(): lax.all_to_all(sending, 'site', split_axis=0, concat_axis=0, tiled=True)]
    dot_general x2 -> x0, matrix products: 25.3 us -> none  [the longest x1 13.4 us: per_device(): jnp.dot(lax.all_gather(u_factors, 'real', axis=1, tiled=True)[0], flatten...]
    dot_general x1 -> x0, local copies, waits for them, and re-layouts: 12 us -> none  [per_device(): lax.dot_general(v_whole, noise, (((0,), (0,)), ((), ())), preferred_eleme...]
    all_to_all x1 -> x0, starting transfers between devices: 9.03 us -> none  [per_device(): lax.all_to_all(sending, 'site', split_axis=0, concat_axis=0, tiled=True)]
    unnamed x6 -> x1, local copies, waits for them, and re-layouts: 0.01 us -> 3.76 us
    mul x1 -> x0, local copies, waits for them, and re-layouts: 3.54 us -> none  [per_device(): jnp.expm1(skew_col * gaussian) / skew_col]
  transfers between devices with their start and end apart: 3 -> 0, of which waited for: 3 -> 0; matrix products, arithmetic and copies ran while one was open for 9% -> 0% of each run, Pallas kernels for 0% -> 0%
where the time goes in v1:
time: 139 us; the launch traced here: 138 us
  Pallas kernels  134 us (96%)
  local copies, waits for them, and re-layouts  3.76 us (3%)
    pallas_call x1, Pallas kernels, per_device(): pl.pallas_call(kernel, out_shape=jax.ShapeDtypeStruct((tile, count), jnp....  134 us
    unnamed x1, local copies, waits for them, and re-layouts  3.76 us

profile of v1, /device:TPU:4, one launch (start us, length us, event | category | flops | bytes accessed | tf_op | source)
XLA Modules:
  0.0 138.1 jit_solution(13612050721528000576)
XLA Ops:
  0.0 134.3 %shard_map.64 = f32[1024,768]{1,0:T(8,128)} custom-call(bf16[1024,768]{1,0:T(8,128)(2,1)} %noise.1, bf16[64,4096]{1,0:T(8,128)(2,1)} %bitcast.4, bf16[64,4096]{1,0:T(8,128)(2,1)} %bitcast.5, s32[16,16]{1,0:T(8,128)} %ranks.1, f32[8,128]{1,0:T(8,128)} %bitcast.6, f32[8,128]{1,0:T(8,128)} %bitcast.7), custom_call_target="tpu_custom_call" | custom-call | tf_op jit(solution)/shard_map/pallas_call | solution.py:325
  134.3 3.8 %copy.8 = f32[1024,768]{1,0:T(8,128)} copy(f32[1024,768]{1,0:T(8,128)} %shard_map.64) | data formatting | bytes 6291456

commit v2 on v1

v2 whole, which is shorter than its diff:
```python
import functools

import jax
import jax.numpy as jnp
from jax import lax
from jax.experimental import pallas as pl
from jax.experimental.pallas import tpu as pltpu
from jax.sharding import PartitionSpec as P

MESH = pl.DeviceIdType.MESH
CAP = 2
ZS = 8
YS = 4
CHUNKS = ((0, 256), (256, 384), (640, 128))

SLOTS = (
    (0, 1, 0), (1, 1, 0), (-1, 1, 0), (2, 1, 0), (-2, 1, 0),
    (-2, 0, 1), (-2, 1, 1), (2, 0, -1),
    (2, 1, -1), (-2, 0, 2), (2, 1, -2),
    (0, 0, 0), (1, 0, 0), (-1, 0, 0), (2, 0, 0), (-2, 0, 0),
)
SENT = 11
EARLY = ((0, 5), (11, 16))
LATE = (5, 11)
AT = {0: 0, 1: 1, -1: 2, 2: 3, -2: 4}
QUARTERS, HALVES = 4, 2


def tukey(x, g, h):
    y = g * x
    series = y * (1.0 + y * (0.5 + y * (1.0 / 6 + y * (1.0 / 24 + y * (1.0 / 120 + y * (1.0 / 720 + y * (1.0 / 5040)))))))
    lifted = jnp.where(jnp.abs(y) < 0.35, series, jnp.exp(y) - 1.0)
    return lifted / g * jnp.exp(0.5 * h * x * x)


def kernel(noise_hbm, v, u, ranks_hbm, skew_hbm, tail_hbm, out_hbm,
           noise, ranks, skew, tail, out, nt, gv, gu, cs, cr, gb, hb,
           vs, vr, as_, ar, ns, nr, ps, pr, local):
    real, site = lax.axis_index("real"), lax.axis_index("site")
    core = lax.rem(real, 2)
    y = lax.rem(lax.div(real, 2), YS)
    xh = lax.div(real, 2 * YS)
    x = lax.div(site, ZS)
    z = lax.rem(site, ZS)
    rows = v.shape[0]
    unit = v.shape[1] // len(SLOTS)
    rank_block = unit // CAP

    def site_of(fx, dz):
        return (1 - x if fx else x) * ZS + lax.rem(z + dz + ZS, ZS)

    def real_of(fh, dy, fc):
        hi = 1 - xh if fh else xh
        lo = 1 - core if fc else core
        return (hi * YS + lax.rem(y + dy + YS, YS)) * 2 + lo

    def cols(index):
        return pl.ds(pl.multiple_of(index * unit, unit), unit)

    def fixed(index):
        return pl.ds(index * unit, unit)

    def part(c):
        return pl.ds(*CHUNKS[c])

    barrier = pltpu.get_barrier_semaphore()
    peers = [(real, site_of(0, d)) for d in (1, -1, 2, -2)]
    peers += [(real, site_of(1, d)) for d in (0, 1, -1, 2, -2)]
    peers += [(real_of(*w), site) for w in ((1, 0, 0), (0, 1, 0), (0, -1, 0), (0, 0, 1))]
    for peer in peers:
        pl.semaphore_signal(barrier, inc=1, device_id=peer, device_id_type=MESH)

    mine = pl.ds(pl.multiple_of(real * rows, rows), rows)
    loads = []

    def load(source, target):
        loads.append(pltpu.make_async_copy(source, target, local.at[len(loads)]))
        loads[-1].start()

    for c in range(len(CHUNKS)):
        load(noise_hbm.at[:, part(c)], noise.at[:, part(c)])
    load(skew_hbm, skew)
    load(tail_hbm, tail)
    load(ranks_hbm, ranks)
    for m, (dj, fx, di) in enumerate(SLOTS):
        if dj == 0:
            load(v.at[:, cols(site_of(fx, di))], gv.at[mine, fixed(m)])
    for m, (dj, fx, di) in enumerate(SLOTS):
        load(u.at[:, cols(site_of(fx, dj - di))], gu.at[mine, fixed(m)])

    v_copies = {}
    for m, (dj, fx, di) in enumerate(SLOTS):
        if dj != 0:
            v_copies[m] = pltpu.make_async_remote_copy(
                src_ref=v.at[:, cols(site_of(fx, di - dj))], dst_ref=gv.at[mine, fixed(m)],
                send_sem=vs.at[m], recv_sem=vr.at[m],
                device_id=(real, site_of(0, -dj)), device_id_type=MESH,
            )

    KINDS = (
        ((0, 0), (1, 0, 0)),
        ((0, 0), (0, 1, 0)), ((0, 0), (0, -1, 0)),
        ((1, 0), (0, 1, 0)), ((1, 0), (0, -1, 0)),
        ((0, -1), (0, 1, 0)), ((1, 1), (0, -1, 0)),
    ) + tuple((block, (0, 0, 1)) for block in ((0, 0), (1, 0), (0, -1), (0, 1), (1, -1), (1, 1), (0, 2), (1, 2)))
    gathers = []

    def gather(buffer, pieces):
        width = buffer.shape[1] // pieces
        for p in range(pieces):
            copies = []
            for kind, ((fh, dy), to) in enumerate(KINDS):
                owner = real_of(fh, dy, 0)
                block = buffer.at[pl.ds(pl.multiple_of(owner * rows, rows), rows), pl.ds(p * width, width)]
                index = len(gathers) * len(KINDS) + kind
                copies.append(
                    pltpu.make_async_remote_copy(
                        src_ref=block, dst_ref=block, send_sem=as_.at[index], recv_sem=ar.at[index],
                        device_id=(real_of(*to), site), device_id_type=MESH,
                    )
                )
            gathers.append(copies)

    gather(gv, QUARTERS)
    gather(gu, HALVES)
    ua, ub = gathers[QUARTERS], gathers[QUARTERS + 1]

    def start(copies, *kinds):
        for kind in kinds:
            copies[kind].start()

    def step(copies, number):
        if number == 0:
            start(copies, 0, 1, 2, 7)
        elif number == 1:
            copies[0].wait_recv()
            start(copies, 3, 4, 8)
        elif number == 2:
            copies[1].wait_recv()
            start(copies, 5, 9)
            copies[2].wait_recv()
            start(copies, 10)
        elif number == 3:
            copies[4].wait_recv()
            start(copies, 6, 12)
            copies[3].wait_recv()
            start(copies, 11)
        elif number == 4:
            copies[5].wait_recv()
            start(copies, 13)
            copies[6].wait_recv()
            start(copies, 14)
        else:
            for kind in range(7, 15):
                copies[kind].wait_recv()

    def steps(*numbers):
        for quarter, number in numbers:
            step(gathers[quarter], number)

    def noise_copy(c, way, hop):
        return pltpu.make_async_remote_copy(
            src_ref=nt.at[0 if hop == 0 else AT[-way], part(c)],
            dst_ref=nt.at[AT[-way * (hop + 1)], part(c)],
            send_sem=ns.at[(c * 2 + (way > 0)) * 2 + hop], recv_sem=nr.at[(c * 2 + (way > 0)) * 2 + hop],
            device_id=(real, site_of(0, way)), device_id_type=MESH,
        )

    noise_copies = {(c, way, hop): noise_copy(c, way, hop) for c in range(len(CHUNKS)) for way in (1, -1) for hop in (0, 1)}

    def turn(c):
        loads[c].wait()
        nt[0, part(c), :] = noise[:, part(c)].T

    def first(c):
        for way in (1, -1):
            noise_copies[c, way, 0].start()

    def forward(c):
        for way in (1, -1):
            noise_copies[c, way, 0].wait_recv()
            noise_copies[c, way, 1].start()

    def far(c):
        for way in (1, -1):
            noise_copies[c, way, 1].wait_recv()

    def coef_copy(m, c):
        dj, fx, di = SLOTS[m]
        return pltpu.make_async_remote_copy(
            src_ref=cs.at[part(c), fixed(m)], dst_ref=cr.at[part(c), fixed(m)],
            send_sem=ps.at[m * len(CHUNKS) + c], recv_sem=pr.at[m * len(CHUNKS) + c],
            device_id=(real, site_of(fx, di)), device_id_type=MESH,
        )

    coef_copies = {(m, c): coef_copy(m, c) for m in range(SENT) for c in range(len(CHUNKS))}
    level = lax.broadcasted_iota(jnp.int32, (1, unit), 1) // rank_block

    def project(m, c):
        dj, fx, di = SLOTS[m]
        projected = jnp.dot(nt[AT[dj], part(c), :], gv[:, fixed(m)], preferred_element_type=jnp.float32)
        alive = (level < ranks[site_of(fx, di), site_of(0, dj)]).astype(jnp.float32)
        (cs if m < SENT else cr)[part(c), fixed(m)] = (projected * alive).astype(jnp.bfloat16)

    def projects(c, *slots):
        waiting = None
        for m in slots:
            project(m, c)
            if waiting is not None:
                coef_copies[waiting, c].start()
            waiting = m if m < SENT else None
        if waiting is not None:
            coef_copies[waiting, c].start()

    def dot_t(left, right):
        return lax.dot_general(left, right, (((1,), (1,)), ((), ())), preferred_element_type=jnp.float32)

    block = 256

    def early(c):
        @pl.loop(0, out.shape[0] // block)
        def _(k):
            here = pl.ds(pl.multiple_of(k * block, block), block)
            total = None
            for lo, hi in EARLY:
                span = pl.ds(lo * unit, (hi - lo) * unit)
                term = dot_t(gu[here, span], cr[part(c), span])
                total = term if total is None else total + term
            out[here, part(c)] = total

    def late(c):
        begin, width = CHUNKS[c]

        @pl.loop(0, out.shape[0] // block)
        def _(k):
            here = pl.ds(pl.multiple_of(k * block, block), block)
            span = pl.ds(LATE[0] * unit, (LATE[1] - LATE[0]) * unit)
            total = out[here, part(c)] + dot_t(gu[here, span], cr[part(c), span])
            g, h = gb[here, :], hb[here, :]
            for q in range(0, width, 128):
                out[here, pl.ds(begin + q, 128)] = tukey(total[:, q:q + 128], g, h)

    stores = [
        pltpu.make_async_copy(out.at[:, part(c)], out_hbm.at[:, part(c)], local.at[len(loads) + c])
        for c in range(len(CHUNKS))
    ]

    def arrived(slots, c):
        for m in slots:
            coef_copies[m, c].wait_recv()

    beside = range(5)
    relayed = range(5, SENT)
    turn(0)
    pl.semaphore_wait(barrier, len(peers))
    for m in v_copies:
        v_copies[m].start()
    turn(1)
    first(0)
    turn(2)
    first(1)
    for copy in loads[len(CHUNKS):]:
        copy.wait()
    start(ua, 0, 7)
    for k in range(skew.shape[0]):
        spread = pl.ds(k * 128, 128)
        gb[spread, :] = jnp.broadcast_to(skew[pl.ds(k, 1), :], (128, 128)).T
        hb[spread, :] = jnp.broadcast_to(tail[pl.ds(k, 1), :], (128, 128)).T

    def ready(quarter):
        count = len(SLOTS) // QUARTERS
        for m in range(quarter * count, (quarter + 1) * count):
            if m in v_copies:
                v_copies[m].wait_recv()
        step(gathers[quarter], 0)

    ready(0)
    steps((0, 1))
    ready(1)
    steps((0, 2), (1, 1))
    ready(2)
    steps((0, 3), (1, 2), (2, 1))
    ready(3)
    start(ub, 0, 7)
    steps((0, 4), (1, 3), (2, 2), (3, 1))
    forward(0)
    first(2)
    steps((0, 5))
    projects(0, 0)
    projects(1, 0)
    steps((1, 4), (2, 3), (3, 2))
    start(ua, 1, 2)
    projects(0, 1, 2)
    steps((1, 5), (2, 4), (3, 3))
    step(ua, 1)
    projects(2, 0)
    forward(1)
    projects(1, 1, 2)
    steps((2, 5), (3, 4))
    step(ua, 2)
    start(ub, 1, 2)
    steps((3, 5))
    far(0)
    projects(0, 9, 10, 5, 6, 7, 8, 3, 4)
    step(ua, 3)
    step(ub, 1)
    forward(2)
    projects(2, 1, 2)
    projects(0, 11, 12, 13, 14, 15)
    step(ua, 4)
    step(ub, 2)
    projects(1, 11, 12, 13)
    projects(2, 11, 12, 13)
    step(ub, 3)
    far(1)
    projects(1, 9, 10, 5, 6, 7, 8, 3, 4)
    step(ub, 4)
    projects(1, 14, 15)
    step(ua, 5)
    step(ub, 5)
    arrived(beside, 0)
    early(0)
    far(2)
    projects(2, 9, 10, 5, 6, 7, 8, 3, 4, 14, 15)
    arrived(relayed, 0)
    late(0)
    stores[0].start()
    arrived(beside, 1)
    early(1)
    arrived(beside, 2)
    early(2)
    arrived(relayed, 1)
    late(1)
    stores[1].start()
    arrived(relayed, 2)
    late(2)
    stores[2].start()

    for copy in v_copies.values():
        copy.wait_send()
    for copies in gathers:
        for copy in copies:
            copy.wait_send()
    for copy in noise_copies.values():
        copy.wait_send()
    for copy in coef_copies.values():
        copy.wait_send()
    for copy in stores:
        copy.wait()


def per_device(noise, v_factors, u_factors, ranks, skew_g, tail_h):
    v, u = v_factors[0], u_factors[0]
    tile, count = noise.shape
    columns = v.shape[1]
    anywhere = pl.BlockSpec(memory_space=pl.ANY)
    dma = pltpu.SemaphoreType.DMA
    gathers = (QUARTERS + HALVES) * 15
    skew, tail = skew_g.reshape(-1, 128), tail_h.reshape(-1, 128)
    return pl.pallas_call(
        kernel,
        out_shape=jax.ShapeDtypeStruct((tile, count), jnp.float32),
        in_specs=[anywhere] * 6,
        out_specs=anywhere,
        scratch_shapes=[
            pltpu.VMEM((tile, count), jnp.bfloat16),
            pltpu.SMEM(ranks.shape, jnp.int32),
            pltpu.VMEM(skew.shape, jnp.float32),
            pltpu.VMEM(tail.shape, jnp.float32),
            pltpu.VMEM((tile, count), jnp.float32),
            pltpu.VMEM((5, count, tile), jnp.bfloat16),
            pltpu.VMEM((tile, columns), jnp.bfloat16),
            pltpu.VMEM((tile, columns), jnp.bfloat16),
            pltpu.VMEM((count, columns // len(SLOTS) * SENT), jnp.bfloat16),
            pltpu.VMEM((count, columns), jnp.bfloat16),
            pltpu.VMEM((tile, 128), jnp.float32),
            pltpu.VMEM((tile, 128), jnp.float32),
            dma((16,)), dma((16,)),
            dma((gathers,)), dma((gathers,)),
            dma((12,)), dma((12,)),
            dma((SENT * 3,)), dma((SENT * 3,)),
            dma((32,)),
        ],
        compiler_params=pltpu.CompilerParams(
            collective_id=0, has_side_effects=True, vmem_limit_bytes=60 * 1024 * 1024
        ),
    )(noise, v, u, ranks, skew, tail)


def solution(mesh):
    placed = (
        P("site", "real"),
        P("site", "real", None),
        P("site", "real", None),
        P(),
        P("site"),
        P("site"),
    )
    return jax.shard_map(
        per_device, mesh=mesh, in_specs=placed, out_specs=P("site", "real"), check_vma=False
    )
```

time: 139 us -> 132 us (0.950)
  Pallas kernels: 134 us -> 127 us
    pallas_call x1, Pallas kernels: 134 us -> 127 us  [per_device(): pl.pallas_call(kernel, out_shape=jax.ShapeDtypeStruct((tile, count), jnp....]
where the time goes in v2:
time: 132 us; the launch traced here: 131 us
  Pallas kernels  127 us (96%)
  local copies, waits for them, and re-layouts  3.76 us (3%)
    pallas_call x1, Pallas kernels, per_device(): pl.pallas_call(kernel, out_shape=jax.ShapeDtypeStruct((tile, count), jnp....  127 us
    unnamed x1, local copies, waits for them, and re-layouts  3.76 us

profile of v2, /device:TPU:4, one launch (start us, length us, event | category | flops | bytes accessed | tf_op | source)
XLA Modules:
  0.0 131.1 jit_solution(410060741056299507)
XLA Ops:
  0.0 127.3 %shard_map.64 = f32[1024,768]{1,0:T(8,128)} custom-call(bf16[1024,768]{1,0:T(8,128)(2,1)} %noise_hbm.1, bf16[64,4096]{1,0:T(8,128)(2,1)} %bitcast.4, bf16[64,4096]{1,0:T(8,128)(2,1)} %bitcast.5, s32[16,16]{1,0:T(8,128)} %ranks_hbm.1, f32[8,128]{1,0:T(8,128)} %bitcast.6, f32[8,128]{1,0:T(8,128)} %bitcast.7), custom_call_target="tpu_custom_call" | custom-call | tf_op jit(solution)/shard_map/pallas_call | solution.py:360
  127.3 3.8 %copy.8 = f32[1024,768]{1,0:T(8,128)} copy(f32[1024,768]{1,0:T(8,128)} %shard_map.64) | data formatting | bytes 6291456

commit v3 on v2

--- a/solution.py
+++ b/solution.py
@@ -33,8 +33,8 @@
     return lifted / g * jnp.exp(0.5 * h * x * x)
 
 
-def kernel(noise_hbm, v, u, ranks_hbm, skew_hbm, tail_hbm, out_hbm,
-           noise, ranks, skew, tail, out, nt, gv, gu, cs, cr, gb, hb,
+def kernel(noise_hbm, v, u, ranks_hbm, skew_hbm, tail_hbm, out,
+           noise, ranks, skew, tail, nt, gv, gu, cs, cr, gb, hb,
            vs, vr, as_, ar, ns, nr, ps, pr, local):
     real, site = lax.axis_index("real"), lax.axis_index("site")
     core = lax.rem(real, 2)
@@ -239,11 +239,6 @@
             g, h = gb[here, :], hb[here, :]
             for q in range(0, width, 128):
                 out[here, pl.ds(begin + q, 128)] = tukey(total[:, q:q + 128], g, h)
-
-    stores = [
-        pltpu.make_async_copy(out.at[:, part(c)], out_hbm.at[:, part(c)], local.at[len(loads) + c])
-        for c in range(len(CHUNKS))
-    ]
 
     def arrived(slots, c):
         for m in slots:
@@ -324,17 +319,14 @@
     projects(2, 9, 10, 5, 6, 7, 8, 3, 4, 14, 15)
     arrived(relayed, 0)
     late(0)
-    stores[0].start()
     arrived(beside, 1)
     early(1)
     arrived(beside, 2)
     early(2)
     arrived(relayed, 1)
     late(1)
-    stores[1].start()
     arrived(relayed, 2)
     late(2)
-    stores[2].start()
 
     for copy in v_copies.values():
         copy.wait_send()
@@ -345,8 +337,6 @@
         copy.wait_send()
     for copy in coef_copies.values():
         copy.wait_send()
-    for copy in stores:
-        copy.wait()
 
 
 def per_device(noise, v_factors, u_factors, ranks, skew_g, tail_h):
@@ -359,15 +349,14 @@
     skew, tail = skew_g.reshape(-1, 128), tail_h.reshape(-1, 128)
     return pl.pallas_call(
         kernel,
-        out_shape=jax.ShapeDtypeStruct((tile, count), jnp.float32),
+        out_shape=pltpu.VMEM((tile, count), jnp.float32),
         in_specs=[anywhere] * 6,
-        out_specs=anywhere,
+        out_specs=pl.BlockSpec(memory_space=pltpu.VMEM),
         scratch_shapes=[
             pltpu.VMEM((tile, count), jnp.bfloat16),
             pltpu.SMEM(ranks.shape, jnp.int32),
             pltpu.VMEM(skew.shape, jnp.float32),
             pltpu.VMEM(tail.shape, jnp.float32),
-            pltpu.VMEM((tile, count), jnp.float32),
             pltpu.VMEM((5, count, tile), jnp.bfloat16),
             pltpu.VMEM((tile, columns), jnp.bfloat16),
             pltpu.VMEM((tile, columns), jnp.bfloat16),

time: 132 us -> 129 us (0.977)
  local copies, waits for them, and re-layouts: 3.76 us -> 1.67 us
    unnamed x1, local copies, waits for them, and re-layouts: 3.76 us -> 1.67 us
where the time goes in v3:
time: 129 us; the launch traced here: 128 us
  Pallas kernels  127 us (98%)
  local copies, waits for them, and re-layouts  1.67 us (1%)
    pallas_call x1, Pallas kernels, per_device(): pl.pallas_call(kernel, out_shape=pltpu.VMEM((tile, count), jnp.float32),...  127 us

profile of v3, /device:TPU:4, one launch (start us, length us, event | category | flops | bytes accessed | tf_op | source)
XLA Modules:
  0.0 128.3 jit_solution(4195808772802948988)
XLA Ops:
  0.0 126.7 %shard_map.64 = f32[1024,768]{1,0:T(8,128)S(1)} custom-call(bf16[1024,768]{1,0:T(8,128)(2,1)} %noise_hbm.1, bf16[64,4096]{1,0:T(8,128)(2,1)} %bitcast.4, bf16[64,4096]{1,0:T(8,128)(2,1)} %bitcast.5, s32[16,16]{1,0:T(8,128)} %ranks_hbm.1, f32[8,128]{1,0:T(8,128)} %bitcast.6, f32[8,128]{1,0:T(8,128)} %bitcast.7), custom_call_target="tpu_custom_call" | custom-call | tf_op jit(solution)/shard_map/pallas_call | solution.py:350
  126.7 1.7 %copy.8 = f32[1024,768]{1,0:T(8,128)} copy(f32[1024,768]{1,0:T(8,128)S(1)} %shard_map.64) | data formatting | bytes 6291456

commit v4 on v3

--- a/solution.py
+++ b/solution.py
@@ -35,7 +35,7 @@
 
 def kernel(noise_hbm, v, u, ranks_hbm, skew_hbm, tail_hbm, out,
            noise, ranks, skew, tail, nt, gv, gu, cs, cr, gb, hb,
-           vs, vr, as_, ar, ns, nr, ps, pr, local):
+           sent, vr, ar, nr, pr, local):
     real, site = lax.axis_index("real"), lax.axis_index("site")
     core = lax.rem(real, 2)
     y = lax.rem(lax.div(real, 2), YS)
@@ -71,29 +71,30 @@
         pl.semaphore_signal(barrier, inc=1, device_id=peer, device_id_type=MESH)
 
     mine = pl.ds(pl.multiple_of(real * rows, rows), rows)
-    loads = []
-
-    def load(source, target):
-        loads.append(pltpu.make_async_copy(source, target, local.at[len(loads)]))
-        loads[-1].start()
-
-    for c in range(len(CHUNKS)):
-        load(noise_hbm.at[:, part(c)], noise.at[:, part(c)])
-    load(skew_hbm, skew)
-    load(tail_hbm, tail)
-    load(ranks_hbm, ranks)
+    resident = [m for m in range(len(SLOTS)) if SLOTS[m][0] == 0]
+
+    def load(source, target, index):
+        copy = pltpu.make_async_copy(source, target, local.at[index])
+        copy.start()
+        return copy
+
+    def take(semaphore, like):
+        pltpu.make_async_copy(like, like, semaphore).wait()
+
+    noise_loads = [load(noise_hbm.at[:, part(c)], noise.at[:, part(c)], c) for c in range(len(CHUNKS))]
+    small_loads = [load(skew_hbm, skew, 3), load(tail_hbm, tail, 4), load(ranks_hbm, ranks, 5)]
+    for m in resident:
+        dj, fx, di = SLOTS[m]
+        load(v.at[:, cols(site_of(fx, di))], gv.at[mine, fixed(m)], 6)
     for m, (dj, fx, di) in enumerate(SLOTS):
-        if dj == 0:
-            load(v.at[:, cols(site_of(fx, di))], gv.at[mine, fixed(m)])
-    for m, (dj, fx, di) in enumerate(SLOTS):
-        load(u.at[:, cols(site_of(fx, dj - di))], gu.at[mine, fixed(m)])
+        load(u.at[:, cols(site_of(fx, dj - di))], gu.at[mine, fixed(m)], 7)
 
     v_copies = {}
     for m, (dj, fx, di) in enumerate(SLOTS):
         if dj != 0:
             v_copies[m] = pltpu.make_async_remote_copy(
                 src_ref=v.at[:, cols(site_of(fx, di - dj))], dst_ref=gv.at[mine, fixed(m)],
-                send_sem=vs.at[m], recv_sem=vr.at[m],
+                send_sem=sent.at[0], recv_sem=vr.at[m * QUARTERS // len(SLOTS)],
                 device_id=(real, site_of(0, -dj)), device_id_type=MESH,
             )
 
@@ -103,73 +104,58 @@
         ((1, 0), (0, 1, 0)), ((1, 0), (0, -1, 0)),
         ((0, -1), (0, 1, 0)), ((1, 1), (0, -1, 0)),
     ) + tuple((block, (0, 0, 1)) for block in ((0, 0), (1, 0), (0, -1), (0, 1), (1, -1), (1, 1), (0, 2), (1, 2)))
+    GROUPS = (0, 1, 1, 2, 2, 3, 3) + (4,) * 8
     gathers = []
-
-    def gather(buffer, pieces):
+    gathered = []
+
+    def gather(buffer, pieces, sender):
         width = buffer.shape[1] // pieces
         for p in range(pieces):
             copies = []
             for kind, ((fh, dy), to) in enumerate(KINDS):
                 owner = real_of(fh, dy, 0)
                 block = buffer.at[pl.ds(pl.multiple_of(owner * rows, rows), rows), pl.ds(p * width, width)]
-                index = len(gathers) * len(KINDS) + kind
+                index = len(gathers) * 5 + GROUPS[kind]
                 copies.append(
                     pltpu.make_async_remote_copy(
-                        src_ref=block, dst_ref=block, send_sem=as_.at[index], recv_sem=ar.at[index],
+                        src_ref=block, dst_ref=block, send_sem=sent.at[sender], recv_sem=ar.at[index],
                         device_id=(real_of(*to), site), device_id_type=MESH,
                     )
                 )
             gathers.append(copies)
-
-    gather(gv, QUARTERS)
-    gather(gu, HALVES)
-    ua, ub = gathers[QUARTERS], gathers[QUARTERS + 1]
-
-    def start(copies, *kinds):
+            gathered.append((buffer, width))
+
+    gather(gv, QUARTERS, 1)
+    gather(gu, HALVES, 2)
+    ua, ub = QUARTERS, QUARTERS + 1
+
+    def start(piece, *kinds):
         for kind in kinds:
-            copies[kind].start()
-
-    def step(copies, number):
-        if number == 0:
-            start(copies, 0, 1, 2, 7)
-        elif number == 1:
-            copies[0].wait_recv()
-            start(copies, 3, 4, 8)
-        elif number == 2:
-            copies[1].wait_recv()
-            start(copies, 5, 9)
-            copies[2].wait_recv()
-            start(copies, 10)
-        elif number == 3:
-            copies[4].wait_recv()
-            start(copies, 6, 12)
-            copies[3].wait_recv()
-            start(copies, 11)
-        elif number == 4:
-            copies[5].wait_recv()
-            start(copies, 13)
-            copies[6].wait_recv()
-            start(copies, 14)
-        else:
-            for kind in range(7, 15):
-                copies[kind].wait_recv()
+            gathers[piece][kind].start()
+
+    def step(piece, number):
+        buffer, width = gathered[piece]
+        if number > 0:
+            blocks = (1, 2, 2, 2, 8)[number - 1]
+            take(ar.at[piece * 5 + number - 1], buffer.at[pl.ds(0, blocks * rows), pl.ds(0, width)])
+        start(piece, *((0, 1, 2, 7), (3, 4, 8), (5, 9, 10), (6, 12, 11), (13, 14), ())[number])
 
     def steps(*numbers):
         for quarter, number in numbers:
-            step(gathers[quarter], number)
+            step(quarter, number)
 
     def noise_copy(c, way, hop):
         return pltpu.make_async_remote_copy(
             src_ref=nt.at[0 if hop == 0 else AT[-way], part(c)],
             dst_ref=nt.at[AT[-way * (hop + 1)], part(c)],
-            send_sem=ns.at[(c * 2 + (way > 0)) * 2 + hop], recv_sem=nr.at[(c * 2 + (way > 0)) * 2 + hop],
+            send_sem=sent.at[3], recv_sem=nr.at[c * 2 + hop],
             device_id=(real, site_of(0, way)), device_id_type=MESH,
         )
 
     noise_copies = {(c, way, hop): noise_copy(c, way, hop) for c in range(len(CHUNKS)) for way in (1, -1) for hop in (0, 1)}
 
     def turn(c):
-        loads[c].wait()
+        noise_loads[c].wait()
         nt[0, part(c), :] = noise[:, part(c)].T
 
     def first(c):
@@ -177,19 +163,18 @@
             noise_copies[c, way, 0].start()
 
     def forward(c):
+        take(nr.at[c * 2], nt.at[pl.ds(1, 2), part(c)])
         for way in (1, -1):
-            noise_copies[c, way, 0].wait_recv()
             noise_copies[c, way, 1].start()
 
     def far(c):
-        for way in (1, -1):
-            noise_copies[c, way, 1].wait_recv()
+        take(nr.at[c * 2 + 1], nt.at[pl.ds(3, 2), part(c)])
 
     def coef_copy(m, c):
         dj, fx, di = SLOTS[m]
         return pltpu.make_async_remote_copy(
             src_ref=cs.at[part(c), fixed(m)], dst_ref=cr.at[part(c), fixed(m)],
-            send_sem=ps.at[m * len(CHUNKS) + c], recv_sem=pr.at[m * len(CHUNKS) + c],
+            send_sem=sent.at[4], recv_sem=pr.at[c * 2 + (m >= LATE[0])],
             device_id=(real, site_of(fx, di)), device_id_type=MESH,
         )
 
@@ -215,7 +200,7 @@
     def dot_t(left, right):
         return lax.dot_general(left, right, (((1,), (1,)), ((), ())), preferred_element_type=jnp.float32)
 
-    block = 256
+    block = 512
 
     def early(c):
         @pl.loop(0, out.shape[0] // block)
@@ -240,23 +225,23 @@
             for q in range(0, width, 128):
                 out[here, pl.ds(begin + q, 128)] = tukey(total[:, q:q + 128], g, h)
 
-    def arrived(slots, c):
-        for m in slots:
-            coef_copies[m, c].wait_recv()
-
-    beside = range(5)
-    relayed = range(5, SENT)
-    turn(0)
+    def arrived(late_slots, c):
+        slots = LATE[1] - LATE[0] if late_slots else LATE[0]
+        take(pr.at[c * 2 + late_slots], cr.at[part(c), pl.ds(0, slots * unit)])
+
+    beside, relayed = 0, 1
     pl.semaphore_wait(barrier, len(peers))
     for m in v_copies:
         v_copies[m].start()
+    turn(0)
     turn(1)
     first(0)
     turn(2)
     first(1)
-    for copy in loads[len(CHUNKS):]:
+    take(local.at[6], gv.at[pl.ds(0, rows), pl.ds(0, len(resident) * unit)])
+    take(local.at[7], gu.at[pl.ds(0, rows), :])
+    for copy in small_loads:
         copy.wait()
-    start(ua, 0, 7)
     for k in range(skew.shape[0]):
         spread = pl.ds(k * 128, 128)
         gb[spread, :] = jnp.broadcast_to(skew[pl.ds(k, 1), :], (128, 128)).T
@@ -264,59 +249,60 @@
 
     def ready(quarter):
         count = len(SLOTS) // QUARTERS
-        for m in range(quarter * count, (quarter + 1) * count):
-            if m in v_copies:
-                v_copies[m].wait_recv()
-        step(gathers[quarter], 0)
+        coming = sum(m in v_copies for m in range(quarter * count, (quarter + 1) * count))
+        take(vr.at[quarter], gv.at[pl.ds(0, rows), pl.ds(0, coming * unit)])
+        step(quarter, 0)
 
     ready(0)
-    steps((0, 1))
+    steps((0, 1), (0, 2))
     ready(1)
-    steps((0, 2), (1, 1))
+    start(ua, 0, 7)
+    steps((0, 3), (1, 1))
     ready(2)
-    steps((0, 3), (1, 2), (2, 1))
+    steps((0, 4), (1, 2), (0, 5))
+    projects(0, 0)
+    projects(1, 0)
+    projects(2, 0)
     ready(3)
-    start(ub, 0, 7)
-    steps((0, 4), (1, 3), (2, 2), (3, 1))
+    steps((1, 3), (2, 1))
     forward(0)
     first(2)
-    steps((0, 5))
-    projects(0, 0)
-    projects(1, 0)
-    steps((1, 4), (2, 3), (3, 2))
+    projects(0, 1, 2)
+    steps((1, 4), (2, 2), (3, 1))
+    steps((1, 5), (2, 3), (3, 2))
     start(ua, 1, 2)
-    projects(0, 1, 2)
-    steps((1, 5), (2, 4), (3, 3))
-    step(ua, 1)
-    projects(2, 0)
+    steps((2, 4), (3, 3), (2, 5))
     forward(1)
     projects(1, 1, 2)
-    steps((2, 5), (3, 4))
+    step(ua, 1)
+    start(ub, 0, 7)
+    steps((3, 4), (3, 5))
     step(ua, 2)
     start(ub, 1, 2)
-    steps((3, 5))
     far(0)
-    projects(0, 9, 10, 5, 6, 7, 8, 3, 4)
+    projects(0, 3, 4)
+    forward(2)
+    projects(0, 9, 10, 5, 6, 7, 8)
     step(ua, 3)
     step(ub, 1)
-    forward(2)
     projects(2, 1, 2)
     projects(0, 11, 12, 13, 14, 15)
+    projects(1, 11, 12, 13)
+    projects(2, 11, 12, 13)
     step(ua, 4)
     step(ub, 2)
-    projects(1, 11, 12, 13)
-    projects(2, 11, 12, 13)
+    far(1)
+    projects(1, 3, 4, 9, 10, 5, 6, 7, 8)
+    far(2)
+    projects(2, 3, 4, 9, 10, 5, 6, 7, 8)
     step(ub, 3)
-    far(1)
-    projects(1, 9, 10, 5, 6, 7, 8, 3, 4)
     step(ub, 4)
-    projects(1, 14, 15)
     step(ua, 5)
     step(ub, 5)
+    projects(1, 14, 15)
+    projects(2, 14, 15)
     arrived(beside, 0)
     early(0)
-    far(2)
-    projects(2, 9, 10, 5, 6, 7, 8, 3, 4, 14, 15)
     arrived(relayed, 0)
     late(0)
     arrived(beside, 1)
@@ -328,15 +314,11 @@
     arrived(relayed, 2)
     late(2)
 
-    for copy in v_copies.values():
-        copy.wait_send()
-    for copies in gathers:
-        for copy in copies:
-            copy.wait_send()
-    for copy in noise_copies.values():
-        copy.wait_send()
-    for copy in coef_copies.values():
-        copy.wait_send()
+    take(sent.at[0], gv.at[pl.ds(0, rows), pl.ds(0, len(v_copies) * unit)])
+    take(sent.at[1], gv.at[pl.ds(0, 15 * rows), :])
+    take(sent.at[2], gu.at[pl.ds(0, 15 * rows), :])
+    take(sent.at[3], nt.at[pl.ds(0, 4)])
+    take(sent.at[4], cs)
 
 
 def per_device(noise, v_factors, u_factors, ranks, skew_g, tail_h):
@@ -345,7 +327,6 @@
     columns = v.shape[1]
     anywhere = pl.BlockSpec(memory_space=pl.ANY)
     dma = pltpu.SemaphoreType.DMA
-    gathers = (QUARTERS + HALVES) * 15
     skew, tail = skew_g.reshape(-1, 128), tail_h.reshape(-1, 128)
     return pl.pallas_call(
         kernel,
@@ -364,11 +345,12 @@
             pltpu.VMEM((count, columns), jnp.bfloat16),
             pltpu.VMEM((tile, 128), jnp.float32),
             pltpu.VMEM((tile, 128), jnp.float32),
-            dma((16,)), dma((16,)),
-            dma((gathers,)), dma((gathers,)),
-            dma((12,)), dma((12,)),
-            dma((SENT * 3,)), dma((SENT * 3,)),
-            dma((32,)),
+            dma((5,)),
+            dma((QUARTERS,)),
+            dma(((QUARTERS + HALVES) * 5,)),
+            dma((2 * len(CHUNKS),)),
+            dma((2 * len(CHUNKS),)),
+            dma((8,)),
         ],
         compiler_params=pltpu.CompilerParams(
             collective_id=0, has_side_effects=True, vmem_limit_bytes=60 * 1024 * 1024

time: 129 us -> 126 us (0.977)
  Pallas kernels: 127 us -> 123 us
    pallas_call x1, Pallas kernels: 127 us -> 123 us  [per_device(): pl.pallas_call(kernel, out_shape=pltpu.VMEM((tile, count), jnp.float32),...]
where the time goes in v4:
time: 126 us; the launch traced here: 125 us
  Pallas kernels  123 us (98%)
  local copies, waits for them, and re-layouts  1.67 us (1%)
    pallas_call x1, Pallas kernels, per_device(): pl.pallas_call(kernel, out_shape=pltpu.VMEM((tile, count), jnp.float32),...  123 us

profile of v4, /device:TPU:4, one launch (start us, length us, event | category | flops | bytes accessed | tf_op | source)
XLA Modules:
  0.0 125.0 jit_solution(10640814735226676587)
XLA Ops:
  0.0 123.4 %shard_map.64 = f32[1024,768]{1,0:T(8,128)S(1)} custom-call(bf16[1024,768]{1,0:T(8,128)(2,1)} %noise_hbm.1, bf16[64,4096]{1,0:T(8,128)(2,1)} %bitcast.4, bf16[64,4096]{1,0:T(8,128)(2,1)} %bitcast.5, s32[16,16]{1,0:T(8,128)} %ranks_hbm.1, f32[8,128]{1,0:T(8,128)} %bitcast.6, f32[8,128]{1,0:T(8,128)} %bitcast.7), custom_call_target="tpu_custom_call" | custom-call | tf_op jit(solution)/shard_map/pallas_call | solution.py:331
  123.4 1.7 %copy.8 = f32[1024,768]{1,0:T(8,128)} copy(f32[1024,768]{1,0:T(8,128)S(1)} %shard_map.64) | data formatting | bytes 6291456

commit v5 on v4

--- a/solution.py
+++ b/solution.py
@@ -11,7 +11,7 @@
 CAP = 2
 ZS = 8
 YS = 4
-CHUNKS = ((0, 256), (256, 384), (640, 128))
+CHUNKS = ((0, 256), (256, 256), (512, 256))
 
 SLOTS = (
     (0, 1, 0), (1, 1, 0), (-1, 1, 0), (2, 1, 0), (-2, 1, 0),
@@ -21,7 +21,7 @@
 )
 SENT = 11
 EARLY = ((0, 5), (11, 16))
-LATE = (5, 11)
+LATE = (5, 9, 11)
 AT = {0: 0, 1: 1, -1: 2, 2: 3, -2: 4}
 QUARTERS, HALVES = 4, 2
 
@@ -64,8 +64,9 @@
         return pl.ds(*CHUNKS[c])
 
     barrier = pltpu.get_barrier_semaphore()
-    peers = [(real, site_of(0, d)) for d in (1, -1, 2, -2)]
-    peers += [(real, site_of(1, d)) for d in (0, 1, -1, 2, -2)]
+    peers = [(real, site_of(1, d)) for d in (2, -2, 1, -1)]
+    peers += [(real, site_of(0, d)) for d in (2, -2, 1, -1)]
+    peers += [(real, site_of(1, 0))]
     peers += [(real_of(*w), site) for w in ((1, 0, 0), (0, 1, 0), (0, -1, 0), (0, 0, 1))]
     for peer in peers:
         pl.semaphore_signal(barrier, inc=1, device_id=peer, device_id_type=MESH)
@@ -174,7 +175,7 @@
         dj, fx, di = SLOTS[m]
         return pltpu.make_async_remote_copy(
             src_ref=cs.at[part(c), fixed(m)], dst_ref=cr.at[part(c), fixed(m)],
-            send_sem=sent.at[4], recv_sem=pr.at[c * 2 + (m >= LATE[0])],
+            send_sem=sent.at[4], recv_sem=pr.at[c * 3 + (m >= LATE[0]) + (m >= LATE[1])],
             device_id=(real, site_of(fx, di)), device_id_type=MESH,
         )
 
@@ -202,34 +203,42 @@
 
     block = 512
 
+    def product(here, c, lo, hi):
+        span = pl.ds(lo * unit, (hi - lo) * unit)
+        return dot_t(gu[here, span], cr[part(c), span])
+
+    def blocks():
+        return pl.loop(0, out.shape[0] // block)
+
+    def rows_of(k):
+        return pl.ds(pl.multiple_of(k * block, block), block)
+
     def early(c):
-        @pl.loop(0, out.shape[0] // block)
+        @blocks()
         def _(k):
-            here = pl.ds(pl.multiple_of(k * block, block), block)
-            total = None
-            for lo, hi in EARLY:
-                span = pl.ds(lo * unit, (hi - lo) * unit)
-                term = dot_t(gu[here, span], cr[part(c), span])
-                total = term if total is None else total + term
-            out[here, part(c)] = total
-
-    def late(c):
+            out[rows_of(k), part(c)] = product(rows_of(k), c, *EARLY[0]) + product(rows_of(k), c, *EARLY[1])
+
+    def middle(c):
+        @blocks()
+        def _(k):
+            out[rows_of(k), part(c)] += product(rows_of(k), c, LATE[1], LATE[2])
+
+    def late(c, first_slot, last_slot=LATE[2]):
         begin, width = CHUNKS[c]
 
-        @pl.loop(0, out.shape[0] // block)
+        @blocks()
         def _(k):
-            here = pl.ds(pl.multiple_of(k * block, block), block)
-            span = pl.ds(LATE[0] * unit, (LATE[1] - LATE[0]) * unit)
-            total = out[here, part(c)] + dot_t(gu[here, span], cr[part(c), span])
+            here = rows_of(k)
+            total = out[here, part(c)] + product(here, c, first_slot, last_slot)
             g, h = gb[here, :], hb[here, :]
             for q in range(0, width, 128):
                 out[here, pl.ds(begin + q, 128)] = tukey(total[:, q:q + 128], g, h)
 
-    def arrived(late_slots, c):
-        slots = LATE[1] - LATE[0] if late_slots else LATE[0]
-        take(pr.at[c * 2 + late_slots], cr.at[part(c), pl.ds(0, slots * unit)])
-
-    beside, relayed = 0, 1
+    def arrived(group, c):
+        slots = (LATE[0], LATE[1] - LATE[0], LATE[2] - LATE[1])[group]
+        take(pr.at[c * 3 + group], cr.at[part(c), pl.ds(0, slots * unit)])
+
+    beside, near, distant = 0, 1, 2
     pl.semaphore_wait(barrier, len(peers))
     for m in v_copies:
         v_copies[m].start()
@@ -255,37 +264,37 @@
 
     ready(0)
     steps((0, 1), (0, 2))
+    start(ua, 0, 7)
+    steps((0, 3))
     ready(1)
-    start(ua, 0, 7)
-    steps((0, 3), (1, 1))
     ready(2)
-    steps((0, 4), (1, 2), (0, 5))
+    steps((0, 4), (0, 5))
     projects(0, 0)
     projects(1, 0)
     projects(2, 0)
     ready(3)
-    steps((1, 3), (2, 1))
+    steps((1, 1), (1, 2))
     forward(0)
     first(2)
     projects(0, 1, 2)
-    steps((1, 4), (2, 2), (3, 1))
-    steps((1, 5), (2, 3), (3, 2))
-    start(ua, 1, 2)
-    steps((2, 4), (3, 3), (2, 5))
+    steps((2, 1), (1, 3), (2, 2), (3, 1))
+    steps((1, 4), (2, 3), (3, 2))
     forward(1)
     projects(1, 1, 2)
+    start(ub, 0, 7)
+    start(ua, 1, 2)
+    steps((1, 5), (2, 4), (3, 3))
+    steps((2, 5), (3, 4), (3, 5))
     step(ua, 1)
-    start(ub, 0, 7)
-    steps((3, 4), (3, 5))
-    step(ua, 2)
     start(ub, 1, 2)
     far(0)
     projects(0, 3, 4)
+    step(ua, 2)
     forward(2)
     projects(0, 9, 10, 5, 6, 7, 8)
+    projects(2, 1, 2)
     step(ua, 3)
     step(ub, 1)
-    projects(2, 1, 2)
     projects(0, 11, 12, 13, 14, 15)
     projects(1, 11, 12, 13)
     projects(2, 11, 12, 13)
@@ -303,16 +312,20 @@
     projects(2, 14, 15)
     arrived(beside, 0)
     early(0)
-    arrived(relayed, 0)
-    late(0)
+    arrived(near, 0)
+    arrived(distant, 0)
+    late(0, LATE[0])
     arrived(beside, 1)
     early(1)
     arrived(beside, 2)
     early(2)
-    arrived(relayed, 1)
-    late(1)
-    arrived(relayed, 2)
-    late(2)
+    arrived(near, 1)
+    arrived(distant, 1)
+    late(1, LATE[0])
+    arrived(distant, 2)
+    middle(2)
+    arrived(near, 2)
+    late(2, LATE[0], LATE[1])
 
     take(sent.at[0], gv.at[pl.ds(0, rows), pl.ds(0, len(v_copies) * unit)])
     take(sent.at[1], gv.at[pl.ds(0, 15 * rows), :])
@@ -349,7 +362,7 @@
             dma((QUARTERS,)),
             dma(((QUARTERS + HALVES) * 5,)),
             dma((2 * len(CHUNKS),)),
-            dma((2 * len(CHUNKS),)),
+            dma((3 * len(CHUNKS),)),
             dma((8,)),
         ],
         compiler_params=pltpu.CompilerParams(

time: 126 us -> 125 us (level)
  no operation moved by 1% of the time
where the time goes in v5:
time: 125 us
  Pallas kernels  123 us (98%)
  local copies, waits for them, and re-layouts  1.67 us (1%)
    pallas_call x1, Pallas kernels, per_device(): pl.pallas_call(kernel, out_shape=pltpu.VMEM((tile, count), jnp.float32),...  123 us

profile of v5, /device:TPU:4, one launch (start us, length us, event | category | flops | bytes accessed | tf_op | source)
XLA Modules:
  0.0 125.1 jit_solution(6435584194543229110)
XLA Ops:
  0.0 123.4 %shard_map.64 = f32[1024,768]{1,0:T(8,128)S(1)} custom-call(bf16[1024,768]{1,0:T(8,128)(2,1)} %noise_hbm.1, bf16[64,4096]{1,0:T(8,128)(2,1)} %bitcast.4, bf16[64,4096]{1,0:T(8,128)(2,1)} %bitcast.5, s32[16,16]{1,0:T(8,128)} %ranks_hbm.1, f32[8,128]{1,0:T(8,128)} %bitcast.6, f32[8,128]{1,0:T(8,128)} %bitcast.7), custom_call_target="tpu_custom_call" | custom-call | tf_op jit(solution)/shard_map/pallas_call | solution.py:344
  123.4 1.7 %copy.8 = f32[1024,768]{1,0:T(8,128)} copy(f32[1024,768]{1,0:T(8,128)S(1)} %shard_map.64) | data formatting | bytes 6291456

commit v6 on v5

--- a/solution.py
+++ b/solution.py
@@ -15,13 +15,13 @@
 
 SLOTS = (
     (0, 1, 0), (1, 1, 0), (-1, 1, 0), (2, 1, 0), (-2, 1, 0),
-    (-2, 0, 1), (-2, 1, 1), (2, 0, -1),
+    (-2, 0, 1), (2, 0, -1), (-2, 1, 1),
     (2, 1, -1), (-2, 0, 2), (2, 1, -2),
     (0, 0, 0), (1, 0, 0), (-1, 0, 0), (2, 0, 0), (-2, 0, 0),
 )
 SENT = 11
 EARLY = ((0, 5), (11, 16))
-LATE = (5, 9, 11)
+LATE = (5, 7, 9, 11)
 AT = {0: 0, 1: 1, -1: 2, 2: 3, -2: 4}
 QUARTERS, HALVES = 4, 2
 
@@ -175,7 +175,7 @@
         dj, fx, di = SLOTS[m]
         return pltpu.make_async_remote_copy(
             src_ref=cs.at[part(c), fixed(m)], dst_ref=cr.at[part(c), fixed(m)],
-            send_sem=sent.at[4], recv_sem=pr.at[c * 3 + (m >= LATE[0]) + (m >= LATE[1])],
+            send_sem=sent.at[4], recv_sem=pr.at[c * 4 + sum(m >= first for first in LATE[:3])],
             device_id=(real, site_of(fx, di)), device_id_type=MESH,
         )
 
@@ -218,27 +218,27 @@
         def _(k):
             out[rows_of(k), part(c)] = product(rows_of(k), c, *EARLY[0]) + product(rows_of(k), c, *EARLY[1])
 
-    def middle(c):
+    def middle(c, group):
         @blocks()
         def _(k):
-            out[rows_of(k), part(c)] += product(rows_of(k), c, LATE[1], LATE[2])
-
-    def late(c, first_slot, last_slot=LATE[2]):
+            out[rows_of(k), part(c)] += product(rows_of(k), c, LATE[group], LATE[group + 1])
+
+    def late(c, start_slot, end):
         begin, width = CHUNKS[c]
 
         @blocks()
         def _(k):
             here = rows_of(k)
-            total = out[here, part(c)] + product(here, c, first_slot, last_slot)
+            total = out[here, part(c)] + product(here, c, start_slot, end)
             g, h = gb[here, :], hb[here, :]
             for q in range(0, width, 128):
                 out[here, pl.ds(begin + q, 128)] = tukey(total[:, q:q + 128], g, h)
 
-    def arrived(group, c):
-        slots = (LATE[0], LATE[1] - LATE[0], LATE[2] - LATE[1])[group]
-        take(pr.at[c * 3 + group], cr.at[part(c), pl.ds(0, slots * unit)])
-
-    beside, near, distant = 0, 1, 2
+    def arrived(c, *groups):
+        for group in groups:
+            slots = LATE[0] if group < 0 else LATE[group + 1] - LATE[group]
+            take(pr.at[c * 4 + group + 1], cr.at[part(c), pl.ds(0, slots * unit)])
+
     pl.semaphore_wait(barrier, len(peers))
     for m in v_copies:
         v_copies[m].start()
@@ -275,57 +275,58 @@
     ready(3)
     steps((1, 1), (1, 2))
     forward(0)
-    first(2)
     projects(0, 1, 2)
     steps((2, 1), (1, 3), (2, 2), (3, 1))
     steps((1, 4), (2, 3), (3, 2))
     forward(1)
+    first(2)
     projects(1, 1, 2)
     start(ub, 0, 7)
     start(ua, 1, 2)
     steps((1, 5), (2, 4), (3, 3))
+    far(0)
+    projects(0, 3, 4)
     steps((2, 5), (3, 4), (3, 5))
     step(ua, 1)
     start(ub, 1, 2)
-    far(0)
-    projects(0, 3, 4)
+    projects(0, 9, 10, 7, 8)
+    far(1)
+    projects(1, 3, 4)
     step(ua, 2)
-    forward(2)
-    projects(0, 9, 10, 5, 6, 7, 8)
-    projects(2, 1, 2)
+    projects(0, 11, 12, 13, 14, 15)
+    projects(1, 11, 12, 13, 14, 15)
     step(ua, 3)
     step(ub, 1)
-    projects(0, 11, 12, 13, 14, 15)
-    projects(1, 11, 12, 13)
+    forward(2)
+    projects(0, 5, 6)
+    projects(1, 9, 10, 5, 6, 7, 8)
+    projects(2, 1, 2)
     projects(2, 11, 12, 13)
     step(ua, 4)
     step(ub, 2)
-    far(1)
-    projects(1, 3, 4, 9, 10, 5, 6, 7, 8)
     far(2)
     projects(2, 3, 4, 9, 10, 5, 6, 7, 8)
     step(ub, 3)
     step(ub, 4)
     step(ua, 5)
     step(ub, 5)
-    projects(1, 14, 15)
     projects(2, 14, 15)
-    arrived(beside, 0)
+    arrived(0, -1)
     early(0)
-    arrived(near, 0)
-    arrived(distant, 0)
-    late(0, LATE[0])
-    arrived(beside, 1)
+    arrived(0, 0, 1, 2)
+    late(0, LATE[0], LATE[3])
+    arrived(1, -1)
     early(1)
-    arrived(beside, 2)
+    arrived(2, -1)
     early(2)
-    arrived(near, 1)
-    arrived(distant, 1)
-    late(1, LATE[0])
-    arrived(distant, 2)
-    middle(2)
-    arrived(near, 2)
-    late(2, LATE[0], LATE[1])
+    arrived(1, 0, 1, 2)
+    late(1, LATE[0], LATE[3])
+    arrived(2, 2)
+    middle(2, 2)
+    arrived(2, 0)
+    middle(2, 0)
+    arrived(2, 1)
+    late(2, LATE[1], LATE[2])
 
     take(sent.at[0], gv.at[pl.ds(0, rows), pl.ds(0, len(v_copies) * unit)])
     take(sent.at[1], gv.at[pl.ds(0, 15 * rows), :])
@@ -362,7 +363,7 @@
             dma((QUARTERS,)),
             dma(((QUARTERS + HALVES) * 5,)),
             dma((2 * len(CHUNKS),)),
-            dma((3 * len(CHUNKS),)),
+            dma((4 * len(CHUNKS),)),
             dma((8,)),
         ],
         compiler_params=pltpu.CompilerParams(

time: 125 us -> 125 us (level)
  no operation moved by 1% of the time
where the time goes in v6:
time: 125 us
  Pallas kernels  123 us (98%)
  local copies, waits for them, and re-layouts  1.67 us (1%)
    pallas_call x1, Pallas kernels, per_device(): pl.pallas_call(kernel, out_shape=pltpu.VMEM((tile, count), jnp.float32),...  123 us

profile of v6, /device:TPU:4, one launch (start us, length us, event | category | flops | bytes accessed | tf_op | source)
XLA Modules:
  0.0 124.7 jit_solution(4541582231796615330)
XLA Ops:
  0.0 123.0 %shard_map.64 = f32[1024,768]{1,0:T(8,128)S(1)} custom-call(bf16[1024,768]{1,0:T(8,128)(2,1)} %noise_hbm.1, bf16[64,4096]{1,0:T(8,128)(2,1)} %bitcast.4, bf16[64,4096]{1,0:T(8,128)(2,1)} %bitcast.5, s32[16,16]{1,0:T(8,128)} %ranks_hbm.1, f32[8,128]{1,0:T(8,128)} %bitcast.6, f32[8,128]{1,0:T(8,128)} %bitcast.7), custom_call_target="tpu_custom_call" | custom-call | tf_op jit(solution)/shard_map/pallas_call | solution.py:345
  123.0 1.7 %copy.8 = f32[1024,768]{1,0:T(8,128)} copy(f32[1024,768]{1,0:T(8,128)S(1)} %shard_map.64) | data formatting | bytes 6291456

commit v7 on v6

--- a/solution.py
+++ b/solution.py
@@ -299,7 +299,7 @@
     step(ub, 1)
     forward(2)
     projects(0, 5, 6)
-    projects(1, 9, 10, 5, 6, 7, 8)
+    projects(1, 9, 10, 7, 8, 5, 6)
     projects(2, 1, 2)
     projects(2, 11, 12, 13)
     step(ua, 4)

time: 125 us -> 125 us (level)
  no operation moved by 1% of the time
where the time goes in v7:
time: 125 us
  Pallas kernels  123 us (98%)
  local copies, waits for them, and re-layouts  1.67 us (1%)
    pallas_call x1, Pallas kernels, per_device(): pl.pallas_call(kernel, out_shape=pltpu.VMEM((tile, count), jnp.float32),...  123 us

profile of v7, /device:TPU:4, one launch (start us, length us, event | category | flops | bytes accessed | tf_op | source)
XLA Modules:
  0.0 124.7 jit_solution(8815094114165880160)
XLA Ops:
  0.0 123.0 %shard_map.64 = f32[1024,768]{1,0:T(8,128)S(1)} custom-call(bf16[1024,768]{1,0:T(8,128)(2,1)} %noise_hbm.1, bf16[64,4096]{1,0:T(8,128)(2,1)} %bitcast.4, bf16[64,4096]{1,0:T(8,128)(2,1)} %bitcast.5, s32[16,16]{1,0:T(8,128)} %ranks_hbm.1, f32[8,128]{1,0:T(8,128)} %bitcast.6, f32[8,128]{1,0:T(8,128)} %bitcast.7), custom_call_target="tpu_custom_call" | custom-call | tf_op jit(solution)/shard_map/pallas_call | solution.py:345
  123.0 1.7 %copy.8 = f32[1024,768]{1,0:T(8,128)} copy(f32[1024,768]{1,0:T(8,128)S(1)} %shard_map.64) | data formatting | bytes 6291456

commit v8 on v7

--- a/solution.py
+++ b/solution.py
@@ -26,15 +26,15 @@
 QUARTERS, HALVES = 4, 2
 
 
-def tukey(x, g, h):
+def tukey(x, g, inverse_g, half_h):
     y = g * x
     series = y * (1.0 + y * (0.5 + y * (1.0 / 6 + y * (1.0 / 24 + y * (1.0 / 120 + y * (1.0 / 720 + y * (1.0 / 5040)))))))
     lifted = jnp.where(jnp.abs(y) < 0.35, series, jnp.exp(y) - 1.0)
-    return lifted / g * jnp.exp(0.5 * h * x * x)
+    return lifted * inverse_g * jnp.exp(half_h * x * x)
 
 
 def kernel(noise_hbm, v, u, ranks_hbm, skew_hbm, tail_hbm, out,
-           noise, ranks, skew, tail, nt, gv, gu, cs, cr, gb, hb,
+           noise, ranks, skew, tail, nt, gv, gu, cs, cr, gb, ib, hb,
            sent, vr, ar, nr, pr, local):
     real, site = lax.axis_index("real"), lax.axis_index("site")
     core = lax.rem(real, 2)
@@ -230,9 +230,9 @@
         def _(k):
             here = rows_of(k)
             total = out[here, part(c)] + product(here, c, start_slot, end)
-            g, h = gb[here, :], hb[here, :]
+            shape = gb[here, :], ib[here, :], hb[here, :]
             for q in range(0, width, 128):
-                out[here, pl.ds(begin + q, 128)] = tukey(total[:, q:q + 128], g, h)
+                out[here, pl.ds(begin + q, 128)] = tukey(total[:, q:q + 128], *shape)
 
     def arrived(c, *groups):
         for group in groups:
@@ -254,7 +254,8 @@
     for k in range(skew.shape[0]):
         spread = pl.ds(k * 128, 128)
         gb[spread, :] = jnp.broadcast_to(skew[pl.ds(k, 1), :], (128, 128)).T
-        hb[spread, :] = jnp.broadcast_to(tail[pl.ds(k, 1), :], (128, 128)).T
+        ib[spread, :] = 1.0 / gb[spread, :]
+        hb[spread, :] = 0.5 * jnp.broadcast_to(tail[pl.ds(k, 1), :], (128, 128)).T
 
     def ready(quarter):
         count = len(SLOTS) // QUARTERS
@@ -359,6 +360,7 @@
             pltpu.VMEM((count, columns), jnp.bfloat16),
             pltpu.VMEM((tile, 128), jnp.float32),
             pltpu.VMEM((tile, 128), jnp.float32),
+            pltpu.VMEM((tile, 128), jnp.float32),
             dma((5,)),
             dma((QUARTERS,)),
             dma(((QUARTERS + HALVES) * 5,)),

time: 125 us -> 125 us (level)
  no operation moved by 1% of the time
where the time goes in v8:
time: 125 us
  Pallas kernels  123 us (98%)
  local copies, waits for them, and re-layouts  1.67 us (1%)
    pallas_call x1, Pallas kernels, per_device(): pl.pallas_call(kernel, out_shape=pltpu.VMEM((tile, count), jnp.float32),...  123 us

profile of v8, /device:TPU:4, one launch (start us, length us, event | category | flops | bytes accessed | tf_op | source)
XLA Modules:
  0.0 124.7 jit_solution(14618252500057153560)
XLA Ops:
  0.0 123.0 %shard_map.64 = f32[1024,768]{1,0:T(8,128)S(1)} custom-call(bf16[1024,768]{1,0:T(8,128)(2,1)} %noise_hbm.1, bf16[64,4096]{1,0:T(8,128)(2,1)} %bitcast.4, bf16[64,4096]{1,0:T(8,128)(2,1)} %bitcast.5, s32[16,16]{1,0:T(8,128)} %ranks_hbm.1, f32[8,128]{1,0:T(8,128)} %bitcast.6, f32[8,128]{1,0:T(8,128)} %bitcast.7), custom_call_target="tpu_custom_call" | custom-call | tf_op jit(solution)/shard_map/pallas_call | solution.py:346
  123.0 1.7 %copy.8 = f32[1024,768]{1,0:T(8,128)} copy(f32[1024,768]{1,0:T(8,128)S(1)} %shard_map.64) | data formatting | bytes 6291456
